TPU v7x, 512 devices: a whole 4x4x16 slice. The times are simulated.
512 devices in a mesh: gx: 64 (over z, y), gz: 8 (over x, core).
Axes of the slice: x: 4, y: 4, z: 16, core: 2. Of those that a mesh axis runs over, the one named last changes fastest.
Arguments:
- tokens: bfloat16 [4, 256, 64, 768], P(None, 'gx', 'gz'), may hold values from -60 to 60
- cross_qkv: bfloat16 [768, 2304], P(None, 'gx'), may hold values from -16 to 16
- cross_out: bfloat16 [768, 768], P('gx'), may hold values from -0.21875 to 0.21875
- depth_qkv: bfloat16 [768, 2304], P(None, 'gx'), may hold values from -16 to 16
- depth_out: bfloat16 [768, 768], P('gx'), may hold values from -0.21875 to 0.21875
- up_proj: bfloat16 [768, 3072], P(None, 'gz'), may hold values from -0.21875 to 0.21875
- down_proj: bfloat16 [3072, 768], P('gz'), may hold values from -0.109375 to 0.109375
- gains: float32 [3, 768], replicated, may hold values from 0.5 to 1.5
- head_weight: float32 [768], replicated, may hold values from -0.21875 to 0.21875
- head_bias: float32 [1], replicated, may hold values from -1 to 1
Outputs:
- features: bfloat16 [4, 256, 64, 768], P(None, 'gx', 'gz')
- geotime: float32 [4, 256, 64], P(None, 'gx', 'gz')
All inputs are finite; a program needn't handle non-finite values.
Results may differ from a plain program's by a relative error of at most 0.013.
Values may be sent and summed in bfloat16 or wider, within the bound.
A program may use at most 64 MiB of HBM per device.

v0:
```python
import math
import jax
import jax.numpy as jnp
from jax import lax
from jax.sharding import PartitionSpec as P

HDIM = 64
log_span = math.log(256.0)


def carried_in(shard, axis, combine, identity):
    peers, position = (lax.axis_size(axis), lax.axis_index(axis))
    everything = lax.all_gather(shard, axis)
    start = jnp.broadcast_to(jnp.asarray(identity, shard.dtype), shard.shape)

    def step(k, before):
        reached = k < position
        new = combine(before, everything[k])
        return jnp.where(reached, new, before)

    return lax.fori_loop(0, peers, step, start)


def encodings(inlines, crosslines, depths, cross_start, depth_start, model_width):
    pairs = model_width // 2
    index = jnp.arange(pairs)
    freq = math.pi * jnp.exp(-log_span * index.astype(jnp.float32) / pairs)
    which = index % 3
    inline_pos = jnp.arange(inlines).astype(jnp.float32)[:, None, None, None]
    cross_pos = (cross_start + jnp.arange(crosslines)).astype(jnp.float32)[None, :, None, None]
    depth_pos = (depth_start + jnp.arange(depths)).astype(jnp.float32)[None, None, :, None]
    zeros = jnp.zeros((inlines, crosslines, depths, pairs), jnp.float32)
    position = jnp.where(
        which == 0, inline_pos + zeros, jnp.where(which == 1, cross_pos + zeros, depth_pos + zeros)
    )
    angle = position * freq
    return jnp.stack([jnp.sin(angle), jnp.cos(angle)], -1).reshape(
        inlines, crosslines, depths, model_width
    )


def normalize(stream, gain):
    scale = lax.rsqrt(jnp.mean(stream * stream, -1, keepdims=True) + 1e-05)
    return (stream * scale * gain).astype(jnp.bfloat16)


def attend(queries, keys, values):
    scale = queries.shape[-1] ** (-0.5)
    scores = (
        jnp.einsum("...qe,...ke->...qk", queries, keys, preferred_element_type=jnp.float32) * scale
    )
    scores = scores - jnp.max(scores, -1, keepdims=True)
    expo = jnp.exp(scores)
    weights = (expo / jnp.sum(expo, -1, keepdims=True)).astype(jnp.bfloat16)
    mixed = jnp.einsum("...qk,...ke->...qe", weights, values, preferred_element_type=jnp.float32)
    return mixed.astype(jnp.bfloat16)


def attend_items(trio):
    return attend(trio[0], trio[1], trio[2])


def body(
    tokens,
    cross_qkv,
    cross_out,
    depth_qkv,
    depth_out,
    up_proj,
    down_proj,
    gains,
    head_weight,
    head_bias,
):
    inlines, cross_dev, depth_dev, model_width = tokens.shape
    tok_rows = inlines * cross_dev * depth_dev
    head_count = model_width // HDIM
    cross_group = lax.axis_size("gx")
    encoding = encodings(
        inlines,
        cross_dev,
        depth_dev,
        lax.axis_index("gx") * cross_dev,
        lax.axis_index("gz") * depth_dev,
        model_width,
    )
    stream = (tokens.astype(jnp.float32) + encoding).reshape(tok_rows, model_width)
    normed = normalize(stream, gains[0])
    packed = jnp.dot(
        normed,
        lax.all_gather(cross_qkv, "gx", axis=1, tiled=True),
        preferred_element_type=jnp.float32,
    ).astype(jnp.bfloat16)
    packed = packed.reshape(inlines, cross_dev, depth_dev, 3, head_count, HDIM)
    lined = jnp.transpose(packed, (3, 0, 2, 4, 1, 5))
    per_item = inlines * depth_dev * head_count // cross_group
    lined = lined.reshape(3, cross_group, per_item, cross_dev, HDIM)
    mixed = attend_items(
        (
            lax.all_to_all(lined[0], "gx", split_axis=0, concat_axis=2, tiled=True),
            lax.all_to_all(lined[1], "gx", split_axis=0, concat_axis=2, tiled=True),
            lax.all_to_all(lined[2], "gx", split_axis=0, concat_axis=2, tiled=True),
        )
    )
    mixed = lax.all_to_all(mixed, "gx", split_axis=2, concat_axis=0, tiled=True)
    mixed = jnp.transpose(
        mixed.reshape(inlines, depth_dev, head_count, cross_dev, HDIM), (0, 3, 1, 2, 4)
    ).reshape(tok_rows, model_width)
    columns = mixed
    stream = stream + jnp.dot(
        columns,
        lax.all_gather(cross_out, "gx", axis=0, tiled=True),
        preferred_element_type=jnp.float32,
    )
    normed = normalize(stream, gains[1])
    packed = jnp.dot(
        normed,
        lax.all_gather(depth_qkv, "gx", axis=1, tiled=True),
        preferred_element_type=jnp.float32,
    ).astype(jnp.bfloat16)
    packed = packed.reshape(inlines, cross_dev, depth_dev, 3, head_count, HDIM)
    lined = jnp.transpose(packed, (3, 0, 1, 4, 2, 5))
    all_keys, all_values = (
        lax.all_gather(lined[1], "gz", axis=3, tiled=True),
        lax.all_gather(lined[2], "gz", axis=3, tiled=True),
    )
    mixed = attend(lined[0], all_keys, all_values)
    mixed = jnp.transpose(mixed, (0, 1, 3, 2, 4)).reshape(tok_rows, model_width)
    columns = mixed
    stream = stream + jnp.dot(
        columns,
        lax.all_gather(depth_out, "gx", axis=0, tiled=True),
        preferred_element_type=jnp.float32,
    )
    normed = normalize(stream, gains[2])
    hidden = jax.nn.gelu(
        jnp.dot(
            lax.all_gather(normed, "gz", axis=0, tiled=True),
            up_proj,
            preferred_element_type=jnp.float32,
        )
    ).astype(jnp.bfloat16)
    stream = stream + lax.psum_scatter(
        jnp.dot(hidden, down_proj, preferred_element_type=jnp.float32).astype(jnp.bfloat16),
        "gz",
        scatter_dimension=0,
        tiled=True,
    ).astype(jnp.float32)
    features = stream.astype(jnp.bfloat16).reshape(inlines, cross_dev, depth_dev, model_width)
    thickness = jax.nn.softplus(
        jnp.dot(stream, head_weight, precision=lax.Precision.HIGHEST) + head_bias[0]
    )
    local_time = jnp.cumsum(thickness.reshape(inlines, cross_dev, depth_dev), axis=2)
    line_total = local_time[:, :, -1]
    carried = carried_in(
        line_total, "gz", lambda earlier, later: earlier + later, jnp.zeros_like(line_total)
    )
    geotime = local_time + carried[:, :, None]
    return (features, geotime)


def solution(mesh):
    return jax.shard_map(
        body,
        mesh=mesh,
        in_specs=(
            P(None, "gx", "gz", None),
            P(None, "gx"),
            P("gx", None),
            P(None, "gx"),
            P("gx", None),
            P(None, "gz"),
            P("gz", None),
            P(),
            P(),
            P(),
        ),
        out_specs=(P(None, "gx", "gz", None), P(None, "gx", "gz")),
        check_vma=False,
    )
```

profile of v0, /device:TPU:1, one launch (start us, length us, event | category | flops | bytes accessed | tf_op | source)
XLA Modules:
  0.0 772.2 jit_solution(6534772506447443359)
XLA Ops:
  7.2 0.7 all-gather.21.cloned.1.call-update
  8.0 0.7 all-gather.23.cloned.1.call-update
  8.7 0.7 all-gather.25.cloned.1.call-update
  9.5 0.8 fusion.41
  10.3 6.4 copy.57
  16.6 4.4 copy.58
  21.4 132.3 %all-gather.21.cloned.1.call-done = bf16[64,36,768]{2,1,0:T(8,128)(2,1)} async-done(((bf16[1,36,768]{2,1,0:T(8,128)(2,1)}), bf16[64,36,768]{2,1,0:T(8,128)(2,1)}) %all-gather.21.cloned.1.call-update) | async-done | bytes 3538960 | tf_op jit(solution)/shard_map/all_gather | solution.py:91
  153.7 6.2 reshape.159
  159.8 3.3 convolution_convert_fusion.1
  163.1 1.0 reshape.145
  164.1 1.1 fusion.53
  165.3 0.3 copy.61
  165.6 0.9 reshape.175
  166.5 8.7 %all-to-all-start.1 = ((bf16[64,2,768]{2,1,0:T(2,128)(2,1)}), bf16[64,2,768]{2,1,0:T(2,128)(2,1)S(1)}, u32[]{:S(2)}, u32[]{:S(2)}) async-start(bf16[64,2,768]{2,1,0:T(2,128)(2,1)} %reshape.175), calls=%async_computation.1 | async-start | bytes 393216 | tf_op jit(solution)/shard_map/all_to_all | solution.py:101
  175.2 0.3 copy.59
  175.5 0.9 reshape.173
  176.5 15.4 %all-to-all-done.1 = bf16[64,2,768]{2,1,0:T(2,128)(2,1)S(1)} async-done(((bf16[64,2,768]{2,1,0:T(2,128)(2,1)}), bf16[64,2,768]{2,1,0:T(2,128)(2,1)S(1)}, u32[]{:S(2)}, u32[]{:S(2)}) %all-to-all-start.1) | async-done | bytes 196640 | tf_op jit(solution)/shard_map/all_to_all | solution.py:101
  191.9 4.6 all-to-all-start
  196.5 0.3 copy.65
  196.8 0.9 reshape.171
  197.7 15.1 %all-to-all-done = bf16[64,2,768]{2,1,0:T(2,128)(2,1)S(1)} async-done(((bf16[64,2,768]{2,1,0:T(2,128)(2,1)}), bf16[64,2,768]{2,1,0:T(2,128)(2,1)S(1)}, u32[]{:S(2)}, u32[]{:S(2)}) %all-to-all-start) | async-done | bytes 196640 | tf_op jit(solution)/shard_map/all_to_all | solution.py:100
  212.9 4.6 all-to-all-start.2
  217.5 0.5 all-gather.27.cloned.1.call-update
  218.1 0.3 reshape.176
  218.5 0.3 reshape.174
  218.9 15.0 %all-to-all-done.2 = bf16[64,2,768]{2,1,0:T(2,128)(2,1)S(1)} async-done(((bf16[64,2,768]{2,1,0:T(2,128)(2,1)}), bf16[64,2,768]{2,1,0:T(2,128)(2,1)S(1)}, u32[]{:S(2)}, u32[]{:S(2)}) %all-to-all-start.2) | async-done | bytes 196640 | tf_op jit(solution)/shard_map/all_to_all | solution.py:102
  234.4 1.8 fusion.55
  236.2 1.7 fusion.27
  237.9 0.3 copy.69
  238.2 1.0 reshape.177
  239.2 4.6 all-to-all-start.3
  244.1 49.5 %all-gather.23.cloned.1.call-done = bf16[64,12,768]{2,1,0:T(8,128)(2,1)} async-done(((bf16[1,12,768]{2,1,0:T(8,128)(2,1)}), bf16[64,12,768]{2,1,0:T(8,128)(2,1)}) %all-gather.23.cloned.1.call-update) | async-done | bytes 1179664 | tf_op jit(solution)/shard_map/all_gather | solution.py:112
  293.6 2.2 reshape.161
  295.9 142.8 %all-gather.25.cloned.1.call-done = bf16[64,36,768]{2,1,0:T(8,128)(2,1)} async-done(((bf16[1,36,768]{2,1,0:T(8,128)(2,1)}), bf16[64,36,768]{2,1,0:T(8,128)(2,1)}) %all-gather.25.cloned.1.call-update) | async-done | bytes 3538960 | tf_op jit(solution)/shard_map/all_gather | solution.py:118
  438.7 6.2 reshape.163
  444.9 0.3 reshape.178
  445.5 0.3 reshape.150
  445.8 0.4 multiply_reduce_fusion.1
  446.2 0.7 copy-done.1
  447.0 3.3 convolution_convert_fusion
  450.3 1.0 reshape.151
  451.3 0.3 copy.84
  451.6 1.0 fusion.54
  452.6 0.5 all-gather.19.cloned.1.call-update
  453.2 122.6 %all-gather.27.cloned.1.call-done = bf16[64,12,768]{2,1,0:T(8,128)(2,1)} async-done(((bf16[1,12,768]{2,1,0:T(8,128)(2,1)}), bf16[64,12,768]{2,1,0:T(8,128)(2,1)}) %all-gather.27.cloned.1.call-update) | async-done | bytes 1179664 | tf_op jit(solution)/shard_map/all_gather | solution.py:132
  575.8 2.2 reshape.165
  578.1 44.5 %all-gather.17.cloned.1.call-done = bf16[1,4,4,12,64,64]{5,4,3,2,1,0:T(8,128)(2,1)} async-done(((bf16[1,4,4,12,8,64]{5,4,3,2,1,0:T(8,128)(2,1)}), bf16[1,4,4,12,64,64]{5,4,3,2,1,0:T(8,128)(2,1)}) %all-gather.17.cloned.1.call-update) | async-done | bytes 1572880 | tf_op jit(solution)/shard_map/all_gather | solution.py:124
  622.5 4.6 fusion.56
  627.2 37.7 %all-gather.19.cloned.1.call-done = bf16[1,4,4,12,64,64]{5,4,3,2,1,0:T(8,128)(2,1)} async-done(((bf16[1,4,4,12,8,64]{5,4,3,2,1,0:T(8,128)(2,1)}), bf16[1,4,4,12,64,64]{5,4,3,2,1,0:T(8,128)(2,1)}) %all-gather.19.cloned.1.call-update) | async-done | bytes 1572880 | tf_op jit(solution)/shard_map/all_gather | solution.py:125
  664.9 3.1 fusion.24
  668.2 0.3 reshape.152
  668.5 0.6 copy-done.2
  669.0 0.4 multiply_reduce_fusion
  669.5 0.8 multiply_convert_fusion
  670.3 33.1 %all-gather.15.cloned.1.call-done = bf16[1024,768]{1,0:T(8,128)(2,1)} async-done(((bf16[128,768]{1,0:T(8,128)(2,1)}), bf16[1024,768]{1,0:T(8,128)(2,1)}) %all-gather.15.cloned.1.call-update) | async-done | bytes 1572880 | tf_op jit(solution)/shard_map/all_gather | solution.py:138
  703.5 4.6 convolution_convert_fusion.2
  708.2 0.7 copy-done.6
  709.5 37.5 %reduce-scatter.2.cloned.1.call-done = bf16[128,768]{1,0:T(8,128)(2,1)} async-done(((bf16[1024,768]{1,0:T(8,128)(2,1)}), bf16[128,768]{1,0:T(8,128)(2,1)}) %reduce-scatter.2.cloned.1.call-update) | async-done | bytes 196624 | tf_op jit(solution)/shard_map/reduce_scatter | solution.py:143
  747.0 1.4 compare_select_fusion
  748.4 0.7 reduce_window_sum.11
  749.3 13.5 %all-gather.2 = f32[32,4,1]{1,2,0:T(1,128)S(1)} all-gather(f32[4,4,1]{1,2,0:T(1,128)S(1)} %copy.75), channel_id=4, replica_groups=mesh['gx'=64,'gz'=8] {'gz'}, dimensions={0}, use_global_device_ids=true | all-gather | bytes 576 | tf_op jit(solution)/shard_map/all_gather | solution.py:13
  762.8 0.3 while.14
  763.1 0.7 broadcast_add_fusion
  763.8 1.6 fusion.37
  (56 shorter events, 2.5 us)
Async XLA Ops:
  7.2 696.3 %copy-start = (bf16[384,768]{1,0:T(8,128)(2,1)S(1)}, bf16[384,768]{1,0:T(8,128)(2,1)}, u32[]{:S(2)}) copy-start(bf16[384,768]{1,0:T(8,128)(2,1)} %param.18) | copy-start | bytes 1769476
  7.2 146.5 %all-gather.21.cloned.1.call-start = ((), (), s32[]{:S(2)}) async-start(), calls=%async_computation.9 | async-start | bytes 3993600 | tf_op jit(solution)/shard_map/all_gather | solution.py:91
  7.9 285.7 %all-gather.23.cloned.1.call-start = ((), (), s32[]{:S(2)}) async-start(), calls=%async_computation.10 | async-start | bytes 1597440 | tf_op jit(solution)/shard_map/all_gather | solution.py:112
  8.7 430.0 %all-gather.25.cloned.1.call-start = ((), (), s32[]{:S(2)}) async-start(), calls=%async_computation.11 | async-start | bytes 3993600 | tf_op jit(solution)/shard_map/all_gather | solution.py:118
  16.6 4.4 copy-start.4
  16.6 4.6 copy-start.5
  165.2 10.0 %copy-start.3 = (bf16[1,4,8,12,4,64]{5,3,0,2,4,1:T(8,128)(2,1)S(1)}, bf16[1,4,8,12,4,64]{5,3,0,2,4,1:T(8,128)(2,1)}, u32[]{:S(2)}) copy-start(bf16[1,4,8,12,4,64]{5,3,0,2,4,1:T(8,128)(2,1)} %get-tuple-element.128) | copy-start | bytes 589828
  166.5 25.4 %all-to-all-start.1 = ((bf16[64,2,768]{2,1,0:T(2,128)(2,1)}), bf16[64,2,768]{2,1,0:T(2,128)(2,1)S(1)}, u32[]{:S(2)}, u32[]{:S(2)}) async-start(bf16[64,2,768]{2,1,0:T(2,128)(2,1)} %reshape.175), calls=%async_computation.1 | async-start | bytes 393216 | tf_op jit(solution)/shard_map/all_to_all | solution.py:101
  191.9 21.0 %all-to-all-start = ((bf16[64,2,768]{2,1,0:T(2,128)(2,1)}), bf16[64,2,768]{2,1,0:T(2,128)(2,1)S(1)}, u32[]{:S(2)}, u32[]{:S(2)}) async-start(bf16[64,2,768]{2,1,0:T(2,128)(2,1)} %reshape.173), calls=%async_computation | async-start | bytes 393216 | tf_op jit(solution)/shard_map/all_to_all | solution.py:100
  212.9 21.1 %all-to-all-start.2 = ((bf16[64,2,768]{2,1,0:T(2,128)(2,1)}), bf16[64,2,768]{2,1,0:T(2,128)(2,1)S(1)}, u32[]{:S(2)}, u32[]{:S(2)}) async-start(bf16[64,2,768]{2,1,0:T(2,128)(2,1)} %reshape.171), calls=%async_computation.2 | async-start | bytes 393216 | tf_op jit(solution)/shard_map/all_to_all | solution.py:102
  217.5 358.3 %all-gather.27.cloned.1.call-start = ((), (), s32[]{:S(2)}) async-start(), calls=%async_computation.12 | async-start | bytes 1597440 | tf_op jit(solution)/shard_map/all_gather | solution.py:132
  239.2 205.6 %all-to-all-start.3 = ((bf16[64,2,768]{2,1,0:T(2,128)(2,1)}), bf16[64,2,768]{2,1,0:T(2,128)(2,1)S(1)}, u32[]{:S(2)}, u32[]{:S(2)}) async-start(bf16[64,2,768]{2,1,0:T(2,128)(2,1)} %reshape.177), calls=%async_computation.3 | async-start | bytes 393216 | tf_op jit(solution)/shard_map/all_to_all | solution.py:105
  243.9 378.7 %all-gather.17.cloned.1.call-start = ((), (), s32[]{:S(2)}) async-start(), calls=%async_computation.7 | async-start | bytes 3538944 | tf_op jit(solution)/shard_map/all_gather | solution.py:124
  446.2 0.7 copy-start.1
  452.6 212.3 %all-gather.19.cloned.1.call-start = ((), (), s32[]{:S(2)}) async-start(), calls=%async_computation.8 | async-start | bytes 3538944 | tf_op jit(solution)/shard_map/all_gather | solution.py:125
  453.2 250.3 %all-gather.15.cloned.1.call-start = ((), (), s32[]{:S(2)}) async-start(), calls=%async_computation.5 | async-start | bytes 1769472 | tf_op jit(solution)/shard_map/all_gather | solution.py:138
  668.0 1.0 copy-start.2
  670.3 76.7 %reduce-scatter.2.cloned.1.call-start = ((), (), s32[]{:S(2)}) async-start(), calls=%async_computation.6 | async-start | bytes 1769472 | tf_op jit(solution)/shard_map/reduce_scatter | solution.py:143
  708.1 0.7 copy-start.6
Sparse Core Ops, SparseCore 0:
  11.0 142.6 all-gather.20
  156.6 136.9 all-gather.22
  296.6 142.0 all-gather.24
  441.5 134.2 all-gather.26
  577.8 44.7 all-gather.16
  624.5 40.3 all-gather.18
  670.4 33.0 all-gather.14
  708.3 38.6 reduce-scatter.1
where the time goes:
time: 773 us; the launch traced here: 772 us
  waiting for transfers between devices  649 us (84%)
  local copies, waits for them, and re-layouts  41.9 us (5%)
  matrix products  24.7 us (3%)
  starting transfers between devices  23.1 us (3%)
  between operations  15.2 us (2%)
  blocking collectives  13.5 us (2%)
    all_gather x1, waiting for transfers between devices, body(): lax.all_gather(depth_qkv, 'gx', axis=1, tiled=True)  143 us
    all_gather x1, waiting for transfers between devices, body(): lax.all_gather(cross_qkv, 'gx', axis=1, tiled=True)  132 us
    all_gather x1, waiting for transfers between devices, body(): lax.all_gather(depth_out, 'gx', axis=0, tiled=True)  123 us
    all_gather x1, waiting for transfers between devices, body(): lax.all_gather(cross_out, 'gx', axis=0, tiled=True)  49.5 us
    all_gather x1, waiting for transfers between devices, body(): lax.all_gather(lined[1], 'gz', axis=3, tiled=True)  44.5 us
    all_gather x1, waiting for transfers between devices, body(): lax.all_gather(lined[2], 'gz', axis=3, tiled=True)  37.7 us
    reduce_scatter x1, waiting for transfers between devices, body(): lax.psum_scatter(jnp.dot(hidden, down_proj, preferred_element_type=jnp.fl...  37.5 us
    all_gather x1, waiting for transfers between devices, body(): lax.all_gather(normed, 'gz', axis=0, tiled=True)  33.1 us
  transfers between devices with their start and end apart: 12, of which 11 were waited for; matrix products, arithmetic and copies ran while one was open for 7% of the time, Pallas kernels for 0%

commit v1 on v0

--- a/solution.py
+++ b/solution.py
@@ -1,11 +1,42 @@
+import functools
 import math
 import jax
 import jax.numpy as jnp
 from jax import lax
 from jax.sharding import PartitionSpec as P
+from jax.lax import axis_index, axis_size, ppermute
 
 HDIM = 64
 log_span = math.log(256.0)
+
+
+def _prepare_sources_all(xs, along_dim):
+    local_out, shaped, block_last = (axis_size("gz"), axis_index("gz"), xs.shape[along_dim])
+    buffers = [s * local_out if ii == along_dim else s for ii, s in enumerate(xs.shape)]
+    big = lax.dynamic_update_slice_in_dim(
+        jnp.zeros(buffers, xs.dtype), xs, shaped * block_last, axis=along_dim
+    )
+    current_arr = local_now = xs
+    c = 1
+    while c < local_out // 2 + 1:
+        current_arr = ppermute(
+            current_arr, "gz", perm=[(ii, (ii + 1) % local_out) for ii in range(local_out)]
+        )
+        big = lax.dynamic_update_slice_in_dim(
+            big, current_arr, (shaped - c) % local_out * block_last, axis=along_dim
+        )
+        if 2 * c < local_out:
+            local_now = ppermute(
+                local_now, "gz", perm=[(ii, (ii - 1) % local_out) for ii in range(local_out)]
+            )
+            big = lax.dynamic_update_slice_in_dim(
+                big, local_now, (shaped + c) % local_out * block_last, axis=along_dim
+            )
+        c += 1
+    return big
+
+
+deliver_links = functools.partial(_prepare_sources_all, along_dim=3)
 
 
 def carried_in(shard, axis, combine, identity):
@@ -121,7 +152,7 @@
     packed = packed.reshape(inlines, cross_dev, depth_dev, 3, head_count, HDIM)
     lined = jnp.transpose(packed, (3, 0, 1, 4, 2, 5))
     all_keys, all_values = (
-        lax.all_gather(lined[1], "gz", axis=3, tiled=True),
+        deliver_links(lined[1]),
         lax.all_gather(lined[2], "gz", axis=3, tiled=True),
     )
     mixed = attend(lined[0], all_keys, all_values)

time: 773 us -> 735 us (0.951)
  waiting for transfers between devices: 649 us -> 580 us
  starting transfers between devices: 23.1 us -> 44.6 us
  local copies, waits for them, and re-layouts: 41.9 us -> 50.8 us
    all_gather x1 -> x0, waiting for transfers between devices: 44.5 us -> none  [body(): lax.all_gather(lined[1], 'gz', axis=3, tiled=True)]
    all_gather x1, waiting for transfers between devices: 37.7 us -> 2.01 us  [body(): lax.all_gather(lined[2], 'gz', axis=3, tiled=True)]
    ppermute x0 -> x7, starting transfers between devices: none -> 21.6 us  [the longest x4 17.5 us: _prepare_sources_all(): ppermute(current_arr, 'gz', perm=[(ii, (ii + 1) % local_out) for ii in ra...]
    ppermute x0 -> x7, waiting for transfers between devices: none -> 10.9 us  [the longest x4 6.5 us: _prepare_sources_all(): ppermute(current_arr, 'gz', perm=[(ii, (ii + 1) % local_out) for ii in ra...]
  transfers between devices with their start and end apart: 12 -> 18, of which waited for: 11 -> 15; matrix products, arithmetic and copies ran while one was open for 7% -> 9% of each run, Pallas kernels for 0% -> 0%
where the time goes in v1:
time: 735 us; the launch traced here: 734 us
  waiting for transfers between devices  580 us (79%)
  local copies, waits for them, and re-layouts  50.8 us (7%)
  starting transfers between devices  44.6 us (6%)
  matrix products  24.7 us (3%)
  between operations  15.3 us (2%)
  blocking collectives  13.4 us (2%)
    all_gather x1, waiting for transfers between devices, body(): lax.all_gather(depth_qkv, 'gx', axis=1, tiled=True)  143 us
    all_gather x1, waiting for transfers between devices, body(): lax.all_gather(cross_qkv, 'gx', axis=1, tiled=True)  132 us
    all_gather x1, waiting for transfers between devices, body(): lax.all_gather(depth_out, 'gx', axis=0, tiled=True)  123 us
    all_gather x1, waiting for transfers between devices, body(): lax.all_gather(cross_out, 'gx', axis=0, tiled=True)  49.9 us
    reduce_scatter x1, waiting for transfers between devices, body(): lax.psum_scatter(jnp.dot(hidden, down_proj, preferred_element_type=jnp.fl...  37.5 us
    all_gather x1, waiting for transfers between devices, body(): lax.all_gather(normed, 'gz', axis=0, tiled=True)  33.2 us
    unnamed x27, local copies, waits for them, and re-layouts  23.8 us
    ppermute x4, starting transfers between devices, _prepare_sources_all(): ppermute(current_arr, 'gz', perm=[(ii, (ii + 1) % local_out) for ii in ra...  17.5 us
  transfers between devices with their start and end apart: 18, of which 15 were waited for; matrix products, arithmetic and copies ran while one was open for 9% of the time, Pallas kernels for 0%

profile of v1, /device:TPU:1, one launch (start us, length us, event | category | flops | bytes accessed | tf_op | source)
XLA Modules:
  0.0 734.0 jit_solution(8789160817267933397)
XLA Ops:
  7.2 0.7 all-gather.17.cloned.1.call-update
  8.0 0.7 all-gather.19.cloned.1.call-update
  8.7 0.7 all-gather.21.cloned.1.call-update
  9.5 0.8 fusion.36
  10.3 6.3 copy.57
  16.6 4.4 copy.58
  21.4 132.3 %all-gather.17.cloned.1.call-done = bf16[64,36,768]{2,1,0:T(8,128)(2,1)} async-done(((bf16[1,36,768]{2,1,0:T(8,128)(2,1)}), bf16[64,36,768]{2,1,0:T(8,128)(2,1)}) %all-gather.17.cloned.1.call-update) | async-done | bytes 3538960 | tf_op jit(solution)/shard_map/all_gather | solution.py:122
  153.7 6.2 reshape.158
  159.9 3.3 convolution_convert_fusion.1
  163.2 1.0 reshape.145
  164.2 1.1 fusion.48
  165.6 0.9 reshape.174
  166.5 8.7 %all-to-all-start.1 = ((bf16[64,2,768]{2,1,0:T(2,128)(2,1)}), bf16[64,2,768]{2,1,0:T(2,128)(2,1)S(1)}, u32[]{:S(2)}, u32[]{:S(2)}) async-start(bf16[64,2,768]{2,1,0:T(2,128)(2,1)} %reshape.174), calls=%async_computation.1 | async-start | bytes 393216 | tf_op jit(solution)/shard_map/all_to_all | solution.py:132
  175.6 0.9 reshape.172
  176.5 15.4 %all-to-all-done.1 = bf16[64,2,768]{2,1,0:T(2,128)(2,1)S(1)} async-done(((bf16[64,2,768]{2,1,0:T(2,128)(2,1)}), bf16[64,2,768]{2,1,0:T(2,128)(2,1)S(1)}, u32[]{:S(2)}, u32[]{:S(2)}) %all-to-all-start.1) | async-done | bytes 196640 | tf_op jit(solution)/shard_map/all_to_all | solution.py:132
  191.9 4.6 all-to-all-start
  196.8 0.9 reshape.170
  197.7 15.1 %all-to-all-done = bf16[64,2,768]{2,1,0:T(2,128)(2,1)S(1)} async-done(((bf16[64,2,768]{2,1,0:T(2,128)(2,1)}), bf16[64,2,768]{2,1,0:T(2,128)(2,1)S(1)}, u32[]{:S(2)}, u32[]{:S(2)}) %all-to-all-start) | async-done | bytes 196640 | tf_op jit(solution)/shard_map/all_to_all | solution.py:131
  212.9 4.6 all-to-all-start.2
  218.9 15.1 %all-to-all-done.2 = bf16[64,2,768]{2,1,0:T(2,128)(2,1)S(1)} async-done(((bf16[64,2,768]{2,1,0:T(2,128)(2,1)}), bf16[64,2,768]{2,1,0:T(2,128)(2,1)S(1)}, u32[]{:S(2)}, u32[]{:S(2)}) %all-to-all-start.2) | async-done | bytes 196640 | tf_op jit(solution)/shard_map/all_to_all | solution.py:133
  234.5 1.8 fusion.49
  236.3 1.7 fusion.22
  238.3 1.0 reshape.176
  239.3 4.6 all-to-all-start.3
  244.2 49.9 %all-gather.19.cloned.1.call-done = bf16[64,12,768]{2,1,0:T(8,128)(2,1)} async-done(((bf16[1,12,768]{2,1,0:T(8,128)(2,1)}), bf16[64,12,768]{2,1,0:T(8,128)(2,1)}) %all-gather.19.cloned.1.call-update) | async-done | bytes 1179664 | tf_op jit(solution)/shard_map/all_gather | solution.py:143
  294.1 2.2 reshape.160
  296.3 142.7 %all-gather.21.cloned.1.call-done = bf16[64,36,768]{2,1,0:T(8,128)(2,1)} async-done(((bf16[1,36,768]{2,1,0:T(8,128)(2,1)}), bf16[64,36,768]{2,1,0:T(8,128)(2,1)}) %all-gather.21.cloned.1.call-update) | async-done | bytes 3538960 | tf_op jit(solution)/shard_map/all_gather | solution.py:149
  439.0 6.2 reshape.162
  446.6 0.7 copy-done.1
  447.3 3.3 convolution_convert_fusion
  450.6 1.0 reshape.151
  451.9 0.8 slice_bitcast_fusion
  452.9 123.2 %all-gather.23.cloned.1.call-done = bf16[64,12,768]{2,1,0:T(8,128)(2,1)} async-done(((bf16[1,12,768]{2,1,0:T(8,128)(2,1)}), bf16[64,12,768]{2,1,0:T(8,128)(2,1)}) %all-gather.23.cloned.1.call-update) | async-done | bytes 1179664 | tf_op jit(solution)/shard_map/all_gather | solution.py:163
  576.1 2.2 reshape.164
  578.4 11.1 %collective-permute-start = (bf16[4,4,12,8,64]{4,3,2,1,0:T(8,128)(2,1)S(1)}, bf16[4,4,12,8,64]{4,3,2,1,0:T(8,128)(2,1)S(1)}, u32[]{:S(2)}, u32[]{:S(2)}) collective-permute-start(bf16[4,4,12,8,64]{4,3,2,1,0:T(8,128)(2,1)S(1)} %get-tuple-element.129), channel_id=1, source_target_pairs={{0,1},{1,2},{2,3},{3,4},{4,5},{5,6},{6,7},{7,0},{8,9},{9,10},{10,1... | collective-permute-start | bytes 589832 | tf_op jit(solution)/shard_map/ppermute | solution.py:22
  589.5 2.5 broadcast_in_dim.11
  592.0 0.8 constant_dynamic-update-slice_fusion.7
  592.8 1.4 collective-permute-done
  594.2 2.5 collective-permute-start.2
  596.8 0.8 constant_dynamic-update-slice_fusion.6
  597.6 0.8 constant_dynamic-update-slice_fusion.5
  598.5 2.9 collective-permute-done.2
  601.4 2.6 collective-permute-start.4
  604.0 1.4 collective-permute-done.3
  605.4 3.9 collective-permute-start.5
  609.3 0.8 constant_dynamic-update-slice_fusion.4
  610.1 0.8 constant_dynamic-update-slice_fusion.3
  610.9 1.4 collective-permute-start.6
  612.3 0.8 constant_dynamic-update-slice_fusion.2
  613.1 3.0 collective-permute-done.5
  616.2 0.8 constant_dynamic-update-slice_fusion.1
  617.0 2.2 collective-permute-done.6
  619.1 0.8 constant_dynamic-update-slice_fusion
  620.0 4.6 fusion.50
  624.6 2.0 all-gather.15.cloned.1.call-done
  626.6 3.1 fusion.19
  631.2 0.8 multiply_convert_fusion
  632.0 33.2 %all-gather.13.cloned.1.call-done = bf16[1024,768]{1,0:T(8,128)(2,1)} async-done(((bf16[128,768]{1,0:T(8,128)(2,1)}), bf16[1024,768]{1,0:T(8,128)(2,1)}) %all-gather.13.cloned.1.call-update) | async-done | bytes 1572880 | tf_op jit(solution)/shard_map/all_gather | solution.py:169
  665.3 4.7 convolution_convert_fusion.2
  671.3 37.5 %reduce-scatter.2.cloned.1.call-done = bf16[128,768]{1,0:T(8,128)(2,1)} async-done(((bf16[1024,768]{1,0:T(8,128)(2,1)}), bf16[128,768]{1,0:T(8,128)(2,1)}) %reduce-scatter.2.cloned.1.call-update) | async-done | bytes 196624 | tf_op jit(solution)/shard_map/reduce_scatter | solution.py:174
  708.8 1.4 compare_select_fusion
  710.2 0.7 reduce_window_sum.11
  711.1 13.4 %all-gather.1 = f32[32,4,1]{1,2,0:T(1,128)S(1)} all-gather(f32[4,4,1]{1,2,0:T(1,128)S(1)} %copy.75), channel_id=3, replica_groups=mesh['gx'=64,'gz'=8] {'gz'}, dimensions={0}, use_global_device_ids=true | all-gather | bytes 576 | tf_op jit(solution)/shard_map/all_gather | solution.py:44
  725.6 1.6 fusion.32
  (76 shorter events, 9.2 us)
Async XLA Ops:
  7.2 658.1 %copy-start = (bf16[384,768]{1,0:T(8,128)(2,1)S(1)}, bf16[384,768]{1,0:T(8,128)(2,1)}, u32[]{:S(2)}) copy-start(bf16[384,768]{1,0:T(8,128)(2,1)} %param.18) | copy-start | bytes 1769476
  7.2 146.5 %all-gather.17.cloned.1.call-start = ((), (), s32[]{:S(2)}) async-start(), calls=%async_computation.8 | async-start | bytes 3993600 | tf_op jit(solution)/shard_map/all_gather | solution.py:122
  7.9 286.1 %all-gather.19.cloned.1.call-start = ((), (), s32[]{:S(2)}) async-start(), calls=%async_computation.9 | async-start | bytes 1597440 | tf_op jit(solution)/shard_map/all_gather | solution.py:143
  8.7 430.4 %all-gather.21.cloned.1.call-start = ((), (), s32[]{:S(2)}) async-start(), calls=%async_computation.10 | async-start | bytes 3993600 | tf_op jit(solution)/shard_map/all_gather | solution.py:149
  16.6 4.4 copy-start.4
  16.6 4.6 copy-start.5
  165.3 10.0 %copy-start.3 = (bf16[1,4,8,12,4,64]{5,3,0,2,4,1:T(8,128)(2,1)S(1)}, bf16[1,4,8,12,4,64]{5,3,0,2,4,1:T(8,128)(2,1)}, u32[]{:S(2)}) copy-start(bf16[1,4,8,12,4,64]{5,3,0,2,4,1:T(8,128)(2,1)} %get-tuple-element.128) | copy-start | bytes 589828
  166.5 25.4 %all-to-all-start.1 = ((bf16[64,2,768]{2,1,0:T(2,128)(2,1)}), bf16[64,2,768]{2,1,0:T(2,128)(2,1)S(1)}, u32[]{:S(2)}, u32[]{:S(2)}) async-start(bf16[64,2,768]{2,1,0:T(2,128)(2,1)} %reshape.174), calls=%async_computation.1 | async-start | bytes 393216 | tf_op jit(solution)/shard_map/all_to_all | solution.py:132
  191.9 21.0 %all-to-all-start = ((bf16[64,2,768]{2,1,0:T(2,128)(2,1)}), bf16[64,2,768]{2,1,0:T(2,128)(2,1)S(1)}, u32[]{:S(2)}, u32[]{:S(2)}) async-start(bf16[64,2,768]{2,1,0:T(2,128)(2,1)} %reshape.172), calls=%async_computation | async-start | bytes 393216 | tf_op jit(solution)/shard_map/all_to_all | solution.py:131
  212.9 21.2 %all-to-all-start.2 = ((bf16[64,2,768]{2,1,0:T(2,128)(2,1)}), bf16[64,2,768]{2,1,0:T(2,128)(2,1)S(1)}, u32[]{:S(2)}, u32[]{:S(2)}) async-start(bf16[64,2,768]{2,1,0:T(2,128)(2,1)} %reshape.170), calls=%async_computation.2 | async-start | bytes 393216 | tf_op jit(solution)/shard_map/all_to_all | solution.py:133
  217.5 358.6 %all-gather.23.cloned.1.call-start = ((), (), s32[]{:S(2)}) async-start(), calls=%async_computation.11 | async-start | bytes 1597440 | tf_op jit(solution)/shard_map/all_gather | solution.py:163
  239.3 205.9 %all-to-all-start.3 = ((bf16[64,2,768]{2,1,0:T(2,128)(2,1)}), bf16[64,2,768]{2,1,0:T(2,128)(2,1)S(1)}, u32[]{:S(2)}, u32[]{:S(2)}) async-start(bf16[64,2,768]{2,1,0:T(2,128)(2,1)} %reshape.176), calls=%async_computation.3 | async-start | bytes 393216 | tf_op jit(solution)/shard_map/all_to_all | solution.py:136
  243.9 382.7 %all-gather.15.cloned.1.call-start = ((), (), s32[]{:S(2)}) async-start(), calls=%async_computation.7 | async-start | bytes 3538944 | tf_op jit(solution)/shard_map/all_gather | solution.py:156
  446.6 0.7 copy-start.1
  452.8 212.5 %all-gather.13.cloned.1.call-start = ((), (), s32[]{:S(2)}) async-start(), calls=%async_computation.5 | async-start | bytes 1769472 | tf_op jit(solution)/shard_map/all_gather | solution.py:169
  578.4 15.8 %collective-permute-start = (bf16[4,4,12,8,64]{4,3,2,1,0:T(8,128)(2,1)S(1)}, bf16[4,4,12,8,64]{4,3,2,1,0:T(8,128)(2,1)S(1)}, u32[]{:S(2)}, u32[]{:S(2)}) collective-permute-start(bf16[4,4,12,8,64]{4,3,2,1,0:T(8,128)(2,1)S(1)} %get-tuple-element.129), channel_id=1, source_target_pairs={{0,1},{1,2},{2,3},{3,4},{4,5},{5,6},{6,7},{7,0},{8,9},{9,10},{10,1... | collective-permute-start | bytes 589832 | tf_op jit(solution)/shard_map/ppermute | solution.py:22
  589.5 7.2 collective-permute-start.1
  594.2 7.2 collective-permute-start.2
  596.7 8.7 %collective-permute-start.3 = (bf16[4,4,12,8,64]{4,3,2,1,0:T(8,128)(2,1)S(1)}, bf16[4,4,12,8,64]{4,3,2,1,0:T(8,128)(2,1)S(1)}, u32[]{:S(2)}, u32[]{:S(2)}) collective-permute-start(bf16[4,4,12,8,64]{4,3,2,1,0:T(8,128)(2,1)S(1)} %collective-permute-done.1), channel_id=1, source_target_pairs={{0,7},{1,0},{2,1},{3,2},{4,3},{5,4},{6,5},{7,6},{8,15},{9,8},{10,9... | collective-permute-start | bytes 589832 | tf_op jit(solution)/shard_map/ppermute | solution.py:29
  601.4 9.5 %collective-permute-start.4 = (bf16[4,4,12,8,64]{4,3,2,1,0:T(8,128)(2,1)S(1)}, bf16[4,4,12,8,64]{4,3,2,1,0:T(8,128)(2,1)S(1)}, u32[]{:S(2)}, u32[]{:S(2)}) collective-permute-start(bf16[4,4,12,8,64]{4,3,2,1,0:T(8,128)(2,1)S(1)} %collective-permute-done.2), channel_id=1, source_target_pairs={{0,1},{1,2},{2,3},{3,4},{4,5},{5,6},{6,7},{7,0},{8,9},{9,10},{10,1... | collective-permute-start | bytes 589832 | tf_op jit(solution)/shard_map/ppermute | solution.py:22
  605.4 10.8 %collective-permute-start.5 = (bf16[4,4,12,8,64]{4,3,2,1,0:T(8,128)(2,1)S(1)}, bf16[4,4,12,8,64]{4,3,2,1,0:T(8,128)(2,1)S(1)}, u32[]{:S(2)}, u32[]{:S(2)}) collective-permute-start(bf16[4,4,12,8,64]{4,3,2,1,0:T(8,128)(2,1)S(1)} %collective-permute-done.3), channel_id=1, source_target_pairs={{0,7},{1,0},{2,1},{3,2},{4,3},{5,4},{6,5},{7,6},{8,15},{9,8},{10,9... | collective-permute-start | bytes 589832 | tf_op jit(solution)/shard_map/ppermute | solution.py:29
  610.9 8.2 %collective-permute-start.6 = (bf16[4,4,12,8,64]{4,3,2,1,0:T(8,128)(2,1)S(1)}, bf16[4,4,12,8,64]{4,3,2,1,0:T(8,128)(2,1)S(1)}, u32[]{:S(2)}, u32[]{:S(2)}) collective-permute-start(bf16[4,4,12,8,64]{4,3,2,1,0:T(8,128)(2,1)S(1)} %collective-permute-done.4), channel_id=1, source_target_pairs={{0,1},{1,2},{2,3},{3,4},{4,5},{5,6},{6,7},{7,0},{8,9},{9,10},{10,1... | collective-permute-start | bytes 589832 | tf_op jit(solution)/shard_map/ppermute | solution.py:22
  629.7 1.0 copy-start.2
  632.0 76.8 %reduce-scatter.2.cloned.1.call-start = ((), (), s32[]{:S(2)}) async-start(), calls=%async_computation.6 | async-start | bytes 1769472 | tf_op jit(solution)/shard_map/reduce_scatter | solution.py:174
  669.9 0.7 copy-start.6
Sparse Core Ops, SparseCore 0:
  11.0 142.6 all-gather.16
  156.6 137.3 all-gather.18
  297.0 141.9 all-gather.20
  441.8 134.2 all-gather.22
  578.1 48.4 all-gather.14
  632.1 33.1 all-gather.12
  670.1 38.6 reduce-scatter.1
